TPU v7x, 32 devices: a whole 2x2x4 slice. The times are simulated.
32 devices in a mesh: gx: 8 (over y, x, core), gy: 4 (over z).
Axes of the slice: x: 2, y: 2, z: 4, core: 2. Of those that a mesh axis runs over, the one named last changes fastest.
Arguments:
- wave_coeffs: bfloat16 [768, 131072], P('gy', 'gx'), may hold values from -6 to 6
- projectors: bfloat16 [256, 131072], P(None, 'gx'), may hold values from -0.0234375 to 0.0234375
- miller_index: int32 [3, 131072], P(None, 'gx'), may hold values from -32 to 31, as said below
- occupations: float32 [768], P('gy'), may hold values from 0 to 2
- species_map: int32 [32], replicated, may hold values from 0 to 3
- proj_counts: int32 [32], replicated, may hold values from 1 to 8, as said below
- onsite_base: float32 [4, 8, 8], replicated, may hold values from -5 to 5
Outputs:
- new_bands: float32 [768, 131072], P('gy', 'gx')
Inputs may be any that keep to these rules, and one draw needn't show every extreme that they name: `miller_index`: each column is a distinct lattice vector; columns run through whole shells of equal squared length in increasing order, the last shell possibly in part. `proj_counts`: some atom has exactly 8 projectors and some atom exactly one.
All inputs are finite; a program needn't handle non-finite values.
Results may differ from a plain program's by a relative error of at most 0.0031.
Values may be sent and summed in bfloat16 or wider, within the bound.
No kernel may reach another device: no remote copies, remote signals or barrier semaphores. Data moves between devices by JAX's collectives and lax.ppermute only.
A program may use at most 64 MiB of HBM per device.

v0:
```python
import jax
import jax.numpy as jnp
from jax import lax
from jax.sharding import PartitionSpec as P

PMAX = 8
ITERS = 2
kinetic_unit = 1.0 / 600.0
hubbard_weight = 2.0
step_length = 0.5


def kinetic_of(miller_index):
    components = miller_index.astype(jnp.float32)
    metric = jnp.array([1.5, 1.0, 0.5], dtype=jnp.float32)
    return jnp.sum(metric[:, None] * components * components, axis=0) * kinetic_unit


def teter_factor(kinetic, band_kinetic):
    scaled_kinetic = kinetic[None, :] / band_kinetic[:, None]
    numerator = 27.0 + scaled_kinetic * (18.0 + scaled_kinetic * (12.0 + 8.0 * scaled_kinetic))
    return numerator / (numerator + 16.0 * scaled_kinetic**4)


def live_table(counts, slot_width):
    slot_index = jnp.arange(slot_width, dtype=jnp.int32)
    return (slot_index[None, :] < counts[:, None]).astype(jnp.float32)


def finish_onsite(masked, density, live_slots, species_rows, onsite_base):
    atom_count, slot_width, band_here = masked.shape
    kind_count = onsite_base.shape[0]
    onehot = (species_rows[:, None] == jnp.arange(kind_count, dtype=jnp.int32)[None, :]).astype(
        jnp.float32
    )
    symmetric = 0.5 * (onsite_base + jnp.swapaxes(onsite_base, 1, 2))
    base_here = jnp.dot(
        onehot,
        symmetric.reshape(kind_count, slot_width * slot_width),
        precision=lax.Precision.HIGHEST,
    ).reshape(atom_count, slot_width, slot_width)
    onsite = base_here + hubbard_weight * density
    return (
        jnp.einsum("apq,aqb->apb", onsite, masked, precision=lax.Precision.HIGHEST)
        * live_slots[:, :, None]
    )


def local(
    wave_coeffs, projectors, miller_index, occupations, species_map, proj_counts, onsite_base
):
    kinetic = kinetic_of(miller_index)
    band_here = wave_coeffs.shape[0]
    band_total = band_here * lax.axis_size("gy")
    atom_total = species_map.shape[0]
    atom_own = atom_total // lax.axis_size("gx")
    own_start = lax.axis_index("gx") * atom_own
    own_species = lax.dynamic_slice_in_dim(species_map, own_start, atom_own, 0)
    own_counts = lax.dynamic_slice_in_dim(proj_counts, own_start, atom_own, 0)
    current = wave_coeffs
    updated = wave_coeffs.astype(jnp.float32)
    for turn_index in range(ITERS):
        values = current.astype(jnp.float32)
        local_norm = jnp.sum(values * values, axis=1)
        local_kin = jnp.sum(kinetic[None, :] * values * values, axis=1)
        operand = current
        held_rows = lax.psum_scatter(
            lax.dot_general(
                projectors, operand, (((1,), (1,)), ((), ())), preferred_element_type=jnp.float32
            ),
            "gx",
            scatter_dimension=0,
            tiled=True,
        )
        raw_proj = held_rows.reshape(-1, PMAX, band_here)
        live_slots = live_table(own_counts, PMAX)
        masked = raw_proj * live_slots[:, :, None]
        local_density = (
            jnp.einsum(
                "apb,aqb->apq",
                masked * occupations[None, None, :],
                masked,
                precision=lax.Precision.HIGHEST,
            )
            / band_total
        )
        density = lax.psum(local_density, "gy")
        weighted = finish_onsite(masked, density, live_slots, own_species, onsite_base)
        weight_bf = weighted.reshape(-1, band_here).astype(jnp.bfloat16)
        weight_cube = weight_bf.astype(jnp.float32).reshape(-1, PMAX, band_here)
        nonlocal_energy = jnp.sum(masked * weight_cube, axis=(0, 1))
        norm_sq, kin_sum, nonlocal_sum = lax.psum((local_norm, local_kin, nonlocal_energy), "gx")
        energy_sum = kin_sum + nonlocal_sum
        nonlocal_part = lax.dot_general(
            lax.all_gather(weight_bf, "gx", axis=0, tiled=True),
            projectors,
            (((0,), (0,)), ((), ())),
            preferred_element_type=jnp.float32,
        )
        applied = kinetic[None, :] * values + nonlocal_part
        eigen_value = energy_sum / norm_sq
        band_kinetic = kin_sum / norm_sq
        residual = applied - eigen_value[:, None] * values
        updated = values - step_length * teter_factor(kinetic, band_kinetic) * residual
        if turn_index + 1 < ITERS:
            current = updated.astype(jnp.bfloat16)
    return updated


def solution(mesh):
    placed = (P("gy", "gx"), P(None, "gx"), P(None, "gx"), P("gy"), P(), P(), P())
    return jax.shard_map(
        local, mesh=mesh, in_specs=placed, out_specs=P("gy", "gx"), check_vma=False
    )
```

profile of v0, /device:TPU:0, one launch (start us, length us, event | category | flops | bytes accessed | tf_op | source)
XLA Modules:
  0.0 216.1 jit_solution(11532262483870975233)
XLA Ops:
  6.6 8.3 %fusion.41 = f32[256,192]{1,0:T(8,128)} fusion(bf16[256,16384]{1,0:T(8,128)(2,1)} %param.9, bf16[192,16384]{1,0:T(8,128)(2,1)} %param.8), kind=kOutput, calls=%fused_computation.70 | convolution fusion | flops 1610612736 | bytes 14876672 | tf_op jit(solution)/shard_map/dot_general | solution.py:68
  15.1 0.3 fusion.13
  15.4 5.4 %fusion.7 = (f32[192]{0:T(256)S(1)}, f32[192]{0:T(256)S(1)}) fusion(bf16[192,16384]{1,0:T(8,128)(2,1)} %param.8, f32[16384]{0:T(1024)S(1)} %broadcast_multiply_fusion), kind=kLoop, calls=%fused_computation.21 | loop fusion | flops 18873984 | bytes 6358528 | tf_op jit(solution)/shard_map/reduce_sum | solution.py:65
  20.8 0.1 dynamic_slice.7
  21.0 0.1 reshape.51
  21.1 0.1 dot_general.35
  21.2 0.2 fusion.17
  21.4 30.2 %reduce-scatter.5.cloned.1.call-done = f32[32,192]{1,0:T(8,128)} async-done(((f32[256,192]{1,0:T(8,128)}), f32[32,192]{1,0:T(8,128)}) %reduce-scatter.5.cloned.1.call-update) | async-done | bytes 24592 | tf_op jit(solution)/shard_map/reduce_scatter | solution.py:67
  51.5 1.1 convolution_multiply_fusion.3
  52.6 18.7 %psum.58 = f32[4,8,8]{2,1,0:T(8,128)S(1)} all-reduce(f32[4,8,8]{2,1,0:T(8,128)S(1)} %convolution_multiply_fusion.3), channel_id=1, replica_groups=mesh['gx'=8,'gy'=4] {'gy'}, use_global_device_ids=true, to_apply=%region_6.0 | all-reduce | flops 256 | bytes 2048 | tf_op jit(solution)/shard_map/psum | solution.py:87
  71.3 1.1 multiply_reduce_fusion.1
  72.4 9.2 %all_gather.6 = bf16[256,192]{1,0:T(8,128)(2,1)S(1)} all-gather(bf16[32,192]{1,0:T(8,128)(2,1)S(1)} %bitcast.44), channel_id=1, replica_groups=mesh['gx'=8,'gy'=4] {'gx'}, dimensions={0}, use_global_device_ids=true | all-gather | bytes 110592 | tf_op jit(solution)/shard_map/all_gather | solution.py:95
  81.6 13.4 %all-reduce.1 = (f32[192]{0:T(256)S(1)}, f32[192]{0:T(256)S(1)}, f32[192]{0:T(256)S(1)}) all-reduce(f32[192]{0:T(256)S(1)} %get-tuple-element.8, f32[192]{0:T(256)S(1)} %get-tuple-element.7, f32[192]{0:T(256)S(1)} %get-tuple-element.19), channel_id=1, replica_groups=mesh['gx'=8,'gy'=4] {'gx'}, use_global_device_ids=true, to_apply=%region_4.0 | all-reduce | flops 576 | bytes 4608 | tf_op jit(solution)/shard_map/psum | solution.py:92
  94.9 15.1 %fusion.9 = (f32[192]{0:T(256)S(1)}, f32[192]{0:T(256)S(1)}, bf16[192,16384]{1,0:T(8,128)(2,1)S(1)}) fusion(f32[16384]{0:T(1024)S(1)} %broadcast_multiply_fusion, f32[192]{0:T(256)S(1)} %get-tuple-element.18, bf16[256,192]{1,0:T(8,128)(2,1)S(1)} %all_gather.6, bf16[256,16384]{1,0:T(8,128)(2,1)} %param.9, f32[192]{0:T(256)S(1)} %get-tuple-element.17, ...), kind=kOutput, calls=%fused_computation.23 | convolution fusion | flops 1695546880 | bytes 21138432 | tf_op jit(solution)/shard_map/dot_general | solution.py:94
  110.0 2.7 %copy-done = bf16[192,16384]{1,0:T(8,128)(2,1)} copy-done((bf16[192,16384]{1,0:T(8,128)(2,1)}, bf16[192,16384]{1,0:T(8,128)(2,1)S(1)}, u32[]{:S(2)}) %copy-start) | copy-done | bytes 6291480
  112.7 6.3 %convolution_bitcast_fusion = f32[256,192]{0,1:T(8,128)S(1)} fusion(bf16[192,16384]{1,0:T(8,128)(2,1)S(1)} %get-tuple-element.21, bf16[256,16384]{1,0:T(8,128)(2,1)} %param.9), kind=kOutput, calls=%fused_computation.25 | convolution fusion | flops 1610612736 | bytes 14876672 | tf_op jit(solution)/shard_map/dot_general | solution.py:68
  119.0 0.8 copy.30
  119.8 30.1 %reduce-scatter.7.cloned.1.call-done = f32[32,192]{1,0:T(8,128)} async-done(((f32[256,192]{1,0:T(8,128)}), f32[32,192]{1,0:T(8,128)}) %reduce-scatter.7.cloned.1.call-update) | async-done | bytes 24592 | tf_op jit(solution)/shard_map/reduce_scatter | solution.py:67
  150.0 1.1 convolution_multiply_fusion.2
  151.1 18.7 %psum.62 = f32[4,8,8]{2,1,0:T(8,128)S(1)} all-reduce(f32[4,8,8]{2,1,0:T(8,128)S(1)} %convolution_multiply_fusion.2), channel_id=1, replica_groups=mesh['gx'=8,'gy'=4] {'gy'}, use_global_device_ids=true, to_apply=%region_14.0 | all-reduce | flops 256 | bytes 2048 | tf_op jit(solution)/shard_map/psum | solution.py:87
  169.8 1.1 multiply_reduce_fusion
  170.9 9.2 %all_gather.7 = bf16[256,192]{1,0:T(8,128)(2,1)S(1)} all-gather(bf16[32,192]{1,0:T(8,128)(2,1)S(1)} %bitcast.43), channel_id=1, replica_groups=mesh['gx'=8,'gy'=4] {'gx'}, dimensions={0}, use_global_device_ids=true | all-gather | bytes 110592 | tf_op jit(solution)/shard_map/all_gather | solution.py:95
  180.0 13.4 %all-reduce = (f32[192]{0:T(256)S(1)}, f32[192]{0:T(256)S(1)}, f32[192]{0:T(256)S(1)}) all-reduce(f32[192]{0:T(256)S(1)} %get-tuple-element.6, f32[192]{0:T(256)S(1)} %get-tuple-element.5, f32[192]{0:T(256)S(1)} %get-tuple-element.22), channel_id=1, replica_groups=mesh['gx'=8,'gy'=4] {'gx'}, use_global_device_ids=true, to_apply=%region_12.0 | all-reduce | flops 576 | bytes 4608 | tf_op jit(solution)/shard_map/psum | solution.py:92
  193.4 15.8 %convert_subtract_fusion = f32[192,16384]{1,0:T(8,128)} fusion(bf16[192,16384]{1,0:T(8,128)(2,1)} %copy-done, bf16[256,192]{1,0:T(8,128)(2,1)S(1)} %all_gather.7, bf16[256,16384]{1,0:T(8,128)(2,1)} %param.9, f32[192]{0:T(256)S(1)} %get-tuple-element.16, f32[192]{0:T(256)S(1)} %get-tuple-element.15, f32[16384]{0:T(1024)S(1)} %broadcast_multiply_fusion), kind=kOutput, calls=%fused_computation | convolution fusion | flops 1673527296 | bytes 27428352 | tf_op jit(solution)/shard_map/dot_general | solution.py:94
  (24 shorter events, 0.4 us)
Async XLA Ops:
  6.5 8.5 %copy-start.3 = (f32[3]{0:T(128)S(1)}, f32[3]{0:T(128)}, u32[]{:S(2)}) copy-start(f32[3]{0:T(128)} %constant.37.clone) | copy-start | bytes 40
  6.5 8.4 %copy-start.2 = (f32[4,8,8]{2,1,0:T(8,128)S(1)}, f32[4,8,8]{2,1,0:T(8,128)}, u32[]{:S(2)}) copy-start(f32[4,8,8]{2,1,0:T(8,128)} %param.14) | copy-start | bytes 3076
  6.5 8.5 %copy-start.1 = (s32[3,16384]{1,0:T(4,128)S(1)}, s32[3,16384]{1,0:T(4,128)}, u32[]{:S(2)}) copy-start(s32[3,16384]{1,0:T(4,128)} %param.10) | copy-start | bytes 589828
  6.5 14.2 %copy-start.5 = (s32[32]{0:T(128)S(1)}, s32[32]{0:T(128)}, u32[]{:S(2)}) copy-start(s32[32]{0:T(128)} %param.13) | copy-start | bytes 388
  6.5 14.4 %copy-start.6 = (s32[32]{0:T(128)S(1)}, s32[32]{0:T(128)}, u32[]{:S(2)}) copy-start(s32[32]{0:T(128)} %param.12) | copy-start | bytes 388
  6.5 45.0 %copy-start.4 = (f32[192]{0:T(256)S(1)}, f32[192]{0:T(256)}, u32[]{:S(2)}) copy-start(f32[192]{0:T(256)} %param.11) | copy-start | bytes 2308
  6.6 45.0 %reduce-scatter.5.cloned.1.call-start = ((), (), s32[]{:S(2)}) async-start(), calls=%async_computation.2 | async-start | bytes 294912 | tf_op jit(solution)/shard_map/reduce_scatter | solution.py:67
  14.9 135.1 %reduce-scatter.7.cloned.1.call-start = ((), (), s32[]{:S(2)}) async-start(), calls=%async_computation.3 | async-start | bytes 294912 | tf_op jit(solution)/shard_map/reduce_scatter | solution.py:67
  110.0 2.7 %copy-start = (bf16[192,16384]{1,0:T(8,128)(2,1)}, bf16[192,16384]{1,0:T(8,128)(2,1)S(1)}, u32[]{:S(2)}) copy-start(bf16[192,16384]{1,0:T(8,128)(2,1)S(1)} %get-tuple-element.21) | copy-start | bytes 18874372
Sparse Core Ops, SparseCore 0:
  15.0 36.4 reduce-scatter.4
  120.0 29.9 reduce-scatter.6
where the time goes:
time: 217 us; the launch traced here: 216 us
  blocking collectives  82.6 us (38%)
  waiting for transfers between devices  60.4 us (28%)
  matrix products  49.9 us (23%)
  between operations  13.5 us (6%)
  other arithmetic  5.76 us (3%)
  local copies, waits for them, and re-layouts  3.89 us (2%)
    reduce_scatter x2, waiting for transfers between devices, local(): lax.psum_scatter(lax.dot_general(projectors, operand, (((1,), (1,)), ((),...  60.3 us
    psum x2, blocking collectives, local(): density = lax.psum(local_density, 'gy')  37.4 us
    dot_general x2, matrix products, local(): lax.dot_general(lax.all_gather(weight_bf, 'gx', axis=0, tiled=True), proj...  30.9 us
    psum x2, blocking collectives, local(): lax.psum((local_norm, local_kin, nonlocal_energy), 'gx')  26.8 us
    all_gather x2, blocking collectives, local(): lax.all_gather(weight_bf, 'gx', axis=0, tiled=True)  18.3 us
    dot_general x2, matrix products, local(): lax.dot_general(projectors, operand, (((1,), (1,)), ((), ())), preferred_...  14.6 us
    reduce_sum x1, other arithmetic, local(): local_kin = jnp.sum(kinetic[None, :] * values * values, axis=1)  5.37 us
  transfers between devices with their start and end apart: 2, of which 2 were waited for; matrix products, arithmetic and copies ran while one was open for 3% of the time, Pallas kernels for 0%

commit v1 on v0

--- a/solution.py
+++ b/solution.py
@@ -84,7 +84,7 @@
             )
             / band_total
         )
-        density = lax.psum(local_density, "gy")
+        density = jnp.sum(lax.all_gather(local_density, "gy"), axis=0)
         weighted = finish_onsite(masked, density, live_slots, own_species, onsite_base)
         weight_bf = weighted.reshape(-1, band_here).astype(jnp.bfloat16)
         weight_cube = weight_bf.astype(jnp.float32).reshape(-1, PMAX, band_here)

time: 217 us -> 208 us (0.959)
  blocking collectives: 82.6 us -> 71.6 us
  waiting for transfers between devices: 60.4 us -> 63.1 us
    psum x2 -> x0, blocking collectives: 37.4 us -> none  [local(): density = lax.psum(local_density, 'gy')]
    all_gather x0 -> x2, blocking collectives: none -> 26.4 us  [local(): density = jnp.sum(lax.all_gather(local_density, 'gy'), axis=0)]
    reduce_scatter x2, waiting for transfers between devices: 60.3 us -> 63 us  [local(): lax.psum_scatter(lax.dot_general(projectors, operand, (((1,), (1,)), ((),...]
where the time goes in v1:
time: 208 us
  blocking collectives  71.6 us (34%)
  waiting for transfers between devices  63.1 us (30%)
  matrix products  49.9 us (24%)
  between operations  13.5 us (6%)
  other arithmetic  5.78 us (3%)
  local copies, waits for them, and re-layouts  3.89 us (2%)
    reduce_scatter x2, waiting for transfers between devices, local(): lax.psum_scatter(lax.dot_general(projectors, operand, (((1,), (1,)), ((),...  63 us
    dot_general x2, matrix products, local(): lax.dot_general(lax.all_gather(weight_bf, 'gx', axis=0, tiled=True), proj...  30.9 us
    psum x2, blocking collectives, local(): lax.psum((local_norm, local_kin, nonlocal_energy), 'gx')  26.8 us
    all_gather x2, blocking collectives, local(): density = jnp.sum(lax.all_gather(local_density, 'gy'), axis=0)  26.4 us
    all_gather x2, blocking collectives, local(): lax.all_gather(weight_bf, 'gx', axis=0, tiled=True)  18.4 us
    dot_general x2, matrix products, local(): lax.dot_general(projectors, operand, (((1,), (1,)), ((), ())), preferred_...  14.6 us
    reduce_sum x1, other arithmetic, local(): local_kin = jnp.sum(kinetic[None, :] * values * values, axis=1)  5.37 us
  transfers between devices with their start and end apart: 2, of which 2 were waited for; matrix products, arithmetic and copies ran while one was open for 3% of the time, Pallas kernels for 0%

profile of v1, /device:TPU:0, one launch (start us, length us, event | category | flops | bytes accessed | tf_op | source)
XLA Modules:
  0.0 207.8 jit_solution(1389517227912603379)
XLA Ops:
  6.6 8.3 %fusion.41 = f32[256,192]{1,0:T(8,128)} fusion(bf16[256,16384]{1,0:T(8,128)(2,1)} %param.9, bf16[192,16384]{1,0:T(8,128)(2,1)} %param.8), kind=kOutput, calls=%fused_computation.70 | convolution fusion | flops 1610612736 | bytes 14876672 | tf_op jit(solution)/shard_map/dot_general | solution.py:68
  15.1 0.3 fusion.13
  15.4 5.4 %fusion.7 = (f32[192]{0:T(256)S(1)}, f32[192]{0:T(256)S(1)}) fusion(bf16[192,16384]{1,0:T(8,128)(2,1)} %param.8, f32[16384]{0:T(1024)S(1)} %broadcast_multiply_fusion), kind=kLoop, calls=%fused_computation.21 | loop fusion | flops 18873984 | bytes 6358528 | tf_op jit(solution)/shard_map/reduce_sum | solution.py:65
  20.8 0.1 dynamic_slice.7
  21.0 0.1 reshape.51
  21.1 0.1 dot_general.35
  21.2 0.2 fusion.17
  21.4 30.2 %reduce-scatter.5.cloned.1.call-done = f32[32,192]{1,0:T(8,128)} async-done(((f32[256,192]{1,0:T(8,128)}), f32[32,192]{1,0:T(8,128)}) %reduce-scatter.5.cloned.1.call-update) | async-done | bytes 24592 | tf_op jit(solution)/shard_map/reduce_scatter | solution.py:67
  51.5 1.1 convolution_multiply_fusion.3
  52.6 13.2 %all-gather = f32[16,8,8]{2,1,0:T(8,128)S(1)} all-gather(f32[4,8,8]{2,1,0:T(8,128)S(1)} %convolution_multiply_fusion.3), channel_id=2, replica_groups=mesh['gx'=8,'gy'=4] {'gy'}, dimensions={0}, use_global_device_ids=true | all-gather | bytes 5120 | tf_op jit(solution)/shard_map/all_gather | solution.py:87
  65.8 1.1 multiply_reduce_fusion.1
  66.9 9.2 %all_gather.20 = bf16[256,192]{1,0:T(8,128)(2,1)S(1)} all-gather(bf16[32,192]{1,0:T(8,128)(2,1)S(1)} %bitcast.48), channel_id=1, replica_groups=mesh['gx'=8,'gy'=4] {'gx'}, dimensions={0}, use_global_device_ids=true | all-gather | bytes 110592 | tf_op jit(solution)/shard_map/all_gather | solution.py:95
  76.1 13.4 %all-reduce.1 = (f32[192]{0:T(256)S(1)}, f32[192]{0:T(256)S(1)}, f32[192]{0:T(256)S(1)}) all-reduce(f32[192]{0:T(256)S(1)} %get-tuple-element.8, f32[192]{0:T(256)S(1)} %get-tuple-element.7, f32[192]{0:T(256)S(1)} %get-tuple-element.19), channel_id=1, replica_groups=mesh['gx'=8,'gy'=4] {'gx'}, use_global_device_ids=true, to_apply=%region_4.0 | all-reduce | flops 576 | bytes 4608 | tf_op jit(solution)/shard_map/psum | solution.py:92
  89.5 15.1 %fusion.9 = (f32[192]{0:T(256)S(1)}, f32[192]{0:T(256)S(1)}, bf16[192,16384]{1,0:T(8,128)(2,1)S(1)}) fusion(f32[16384]{0:T(1024)S(1)} %broadcast_multiply_fusion, f32[192]{0:T(256)S(1)} %get-tuple-element.18, bf16[256,192]{1,0:T(8,128)(2,1)S(1)} %all_gather.20, bf16[256,16384]{1,0:T(8,128)(2,1)} %param.9, f32[192]{0:T(256)S(1)} %get-tuple-element.17, ...), kind=kOutput, calls=%fused_computation.23 | convolution fusion | flops 1695546880 | bytes 21138432 | tf_op jit(solution)/shard_map/dot_general | solution.py:94
  104.6 2.7 %copy-done = bf16[192,16384]{1,0:T(8,128)(2,1)} copy-done((bf16[192,16384]{1,0:T(8,128)(2,1)}, bf16[192,16384]{1,0:T(8,128)(2,1)S(1)}, u32[]{:S(2)}) %copy-start) | copy-done | bytes 6291480
  107.2 6.3 %convolution_bitcast_fusion = f32[256,192]{0,1:T(8,128)S(1)} fusion(bf16[192,16384]{1,0:T(8,128)(2,1)S(1)} %get-tuple-element.21, bf16[256,16384]{1,0:T(8,128)(2,1)} %param.9), kind=kOutput, calls=%fused_computation.25 | convolution fusion | flops 1610612736 | bytes 14876672 | tf_op jit(solution)/shard_map/dot_general | solution.py:68
  113.5 0.8 copy.30
  114.4 32.8 %reduce-scatter.7.cloned.1.call-done = f32[32,192]{1,0:T(8,128)} async-done(((f32[256,192]{1,0:T(8,128)}), f32[32,192]{1,0:T(8,128)}) %reduce-scatter.7.cloned.1.call-update) | async-done | bytes 24592 | tf_op jit(solution)/shard_map/reduce_scatter | solution.py:67
  147.2 1.1 convolution_multiply_fusion.2
  148.3 13.2 %all-gather.1 = f32[16,8,8]{2,1,0:T(8,128)S(1)} all-gather(f32[4,8,8]{2,1,0:T(8,128)S(1)} %convolution_multiply_fusion.2), channel_id=3, replica_groups=mesh['gx'=8,'gy'=4] {'gy'}, dimensions={0}, use_global_device_ids=true | all-gather | bytes 5120 | tf_op jit(solution)/shard_map/all_gather | solution.py:87
  161.5 1.1 multiply_reduce_fusion
  162.6 9.2 %all_gather.23 = bf16[256,192]{1,0:T(8,128)(2,1)S(1)} all-gather(bf16[32,192]{1,0:T(8,128)(2,1)S(1)} %bitcast.47), channel_id=1, replica_groups=mesh['gx'=8,'gy'=4] {'gx'}, dimensions={0}, use_global_device_ids=true | all-gather | bytes 110592 | tf_op jit(solution)/shard_map/all_gather | solution.py:95
  171.8 13.4 %all-reduce = (f32[192]{0:T(256)S(1)}, f32[192]{0:T(256)S(1)}, f32[192]{0:T(256)S(1)}) all-reduce(f32[192]{0:T(256)S(1)} %get-tuple-element.6, f32[192]{0:T(256)S(1)} %get-tuple-element.5, f32[192]{0:T(256)S(1)} %get-tuple-element.22), channel_id=1, replica_groups=mesh['gx'=8,'gy'=4] {'gx'}, use_global_device_ids=true, to_apply=%region_12.0 | all-reduce | flops 576 | bytes 4608 | tf_op jit(solution)/shard_map/psum | solution.py:92
  185.2 15.8 %convert_subtract_fusion = f32[192,16384]{1,0:T(8,128)} fusion(bf16[192,16384]{1,0:T(8,128)(2,1)} %copy-done, bf16[256,192]{1,0:T(8,128)(2,1)S(1)} %all_gather.23, bf16[256,16384]{1,0:T(8,128)(2,1)} %param.9, f32[192]{0:T(256)S(1)} %get-tuple-element.16, f32[192]{0:T(256)S(1)} %get-tuple-element.15, f32[16384]{0:T(1024)S(1)} %broadcast_multiply_fusion), kind=kOutput, calls=%fused_computation | convolution fusion | flops 1673527296 | bytes 27428352 | tf_op jit(solution)/shard_map/dot_general | solution.py:94
  (26 shorter events, 0.4 us)
Async XLA Ops:
  6.5 8.5 %copy-start.3 = (f32[3]{0:T(128)S(1)}, f32[3]{0:T(128)}, u32[]{:S(2)}) copy-start(f32[3]{0:T(128)} %constant.37.clone) | copy-start | bytes 40
  6.5 8.4 %copy-start.2 = (f32[4,8,8]{2,1,0:T(8,128)S(1)}, f32[4,8,8]{2,1,0:T(8,128)}, u32[]{:S(2)}) copy-start(f32[4,8,8]{2,1,0:T(8,128)} %param.14) | copy-start | bytes 3076
  6.5 8.5 %copy-start.1 = (s32[3,16384]{1,0:T(4,128)S(1)}, s32[3,16384]{1,0:T(4,128)}, u32[]{:S(2)}) copy-start(s32[3,16384]{1,0:T(4,128)} %param.10) | copy-start | bytes 589828
  6.5 14.2 %copy-start.5 = (s32[32]{0:T(128)S(1)}, s32[32]{0:T(128)}, u32[]{:S(2)}) copy-start(s32[32]{0:T(128)} %param.13) | copy-start | bytes 388
  6.5 14.4 %copy-start.6 = (s32[32]{0:T(128)S(1)}, s32[32]{0:T(128)}, u32[]{:S(2)}) copy-start(s32[32]{0:T(128)} %param.12) | copy-start | bytes 388
  6.5 45.0 %copy-start.4 = (f32[192]{0:T(256)S(1)}, f32[192]{0:T(256)}, u32[]{:S(2)}) copy-start(f32[192]{0:T(256)} %param.11) | copy-start | bytes 2308
  6.6 45.0 %reduce-scatter.5.cloned.1.call-start = ((), (), s32[]{:S(2)}) async-start(), calls=%async_computation.2 | async-start | bytes 294912 | tf_op jit(solution)/shard_map/reduce_scatter | solution.py:67
  14.9 132.3 %reduce-scatter.7.cloned.1.call-start = ((), (), s32[]{:S(2)}) async-start(), calls=%async_computation.3 | async-start | bytes 294912 | tf_op jit(solution)/shard_map/reduce_scatter | solution.py:67
  104.6 2.7 %copy-start = (bf16[192,16384]{1,0:T(8,128)(2,1)}, bf16[192,16384]{1,0:T(8,128)(2,1)S(1)}, u32[]{:S(2)}) copy-start(bf16[192,16384]{1,0:T(8,128)(2,1)S(1)} %get-tuple-element.21) | copy-start | bytes 18874372
Sparse Core Ops, SparseCore 0:
  15.0 36.4 reduce-scatter.4
  114.5 32.6 reduce-scatter.6
